TPU v7x, 32 devices: a whole 2x2x4 slice. The times are simulated.
32 devices in a mesh: shot: 16 (over z, y, core), surf: 2 (over x).
Axes of the slice: x: 2, y: 2, z: 4, core: 2. Of those that a mesh axis runs over, the one named last changes fastest.
Arguments:
- data: float32 [32, 256, 512], P('shot', 'surf'), may hold values from -6 to 6
- positions: int32 [256], P('surf'), may hold values from 0 to 63, as said below
- plan: int32 [16], replicated, may hold values from 0 to 15, each once
- primaries: bfloat16 [64, 16, 16, 256], P('surf', None, 'shot'), may hold values from -0.03125 to 0.03125
- scale: float32 [32], P('shot'), may hold values from 0.5 to 1.5
Outputs:
- demultiplied: float32 [32, 256, 512], P('shot', 'surf')
Inputs may be any that keep to these rules, and one draw needn't show every extreme that they name: `positions`: receiver r lies at a position of the block [b * 32, (b + 1) * 32) with b = r // 128; in each such block of receivers the first maps to the block's first position and the last to its last. A permutation: slot i of primaries holds receiver panel plan[i].
All inputs are finite; a program needn't handle non-finite values.
Results may differ from a plain program's by a relative error of at most 0.0065.
Values may be sent and summed in bfloat16 or wider, within the bound.
A program may use at most 128 MiB of HBM per device.

v0:
```python
import functools
import math

import jax
import jax.numpy as jnp
import ml_dtypes
import numpy as np
from jax import lax
from jax.experimental import pallas as pl
from jax.experimental.pallas import tpu as pltpu
from jax.sharding import PartitionSpec as P

MESH = pl.DeviceIdType.MESH
F32 = jnp.float32
BF16 = jnp.bfloat16
UNROLL = 16
LAG = 2


def fourier_matrices(samples):
    length = 2 * samples
    index = np.arange(samples)
    angles = (index[:, None] * index[None, :] % length) * (2.0 * math.pi / length)
    cosine, sine = np.cos(angles), np.sin(angles)
    alternate = 1.0 - 2.0 * (index % 2)
    forward_imag = -sine
    forward_imag[:, 0] = alternate
    forward = np.concatenate([cosine, forward_imag], axis=1)
    weights = np.where(index == 0, 1.0, 2.0) / length
    weights = np.concatenate([weights, weights])
    inverse = forward.T * weights[:, None]
    return forward.astype(ml_dtypes.bfloat16), inverse.astype(ml_dtypes.bfloat16)


def chip_at(place, chips):
    half = chips // 2
    side = place // half
    return 2 * (place + side * (chips - 1 - 2 * place)) + side


def kernel(
    sizes,
    plan_ref, scale_ref, where_ref, positions_ref, data_ref, primaries_ref, forward_hbm, inverse_hbm,
    out_ref,
    forward_ref, inverse_ref, gathered, partner, e1, e2, e3, factors, spectrum,
    crossing, crossed, leaving, arrived,
    load_sems, panel_sems, ring_send, ring_recv, cross_send, cross_recv, leave_send, leave_recv,
):
    chips, surfs, shots, depth, width, samples, taps = sizes
    per_surf = width // surfs
    panels = 2 * chips
    shot = lax.axis_index("shot")
    surf = lax.axis_index("surf")
    chip, core = shot // 2, shot % 2
    height, side = chip // 2, chip % 2
    place = height + side * (chips - 1 - 2 * height)
    right = chip_at((place + 1) % chips, chips) * 2 + core
    left = chip_at((place + chips - 1) % chips, chips) * 2 + core

    barrier = pltpu.get_barrier_semaphore()
    pl.semaphore_signal(barrier, inc=1, device_id=(chip * 2 + 1 - core, surf), device_id_type=MESH)

    for to in (right, left):
        pl.semaphore_signal(barrier, inc=1, device_id=(to, surf), device_id_type=MESH)
    for h in range(surfs):

        @pl.when(h != surf)
        def _():
            pl.semaphore_signal(barrier, inc=1, device_id=(shot, h), device_id_type=MESH)

    load_forward = pltpu.make_async_copy(forward_hbm, forward_ref, load_sems.at[0])
    load_inverse = pltpu.make_async_copy(inverse_hbm, inverse_ref, load_sems.at[1])
    load_forward.start()
    load_inverse.start()

    local = positions_ref[...] - surf * depth
    onehot = jnp.where(
        lax.broadcasted_iota(jnp.int32, (depth, local.shape[1]), 0) == local, 1.0, 0.0
    ).astype(BF16)
    for s in range(shots):
        value = data_ref[s]
        top = value.astype(BF16)
        rest = value - top.astype(F32)
        middle = rest.astype(BF16)
        low = (rest - middle.astype(F32)).astype(BF16)
        total = (
            jnp.dot(onehot, top, preferred_element_type=F32)
            + jnp.dot(onehot, middle, preferred_element_type=F32)
            + jnp.dot(onehot, low, preferred_element_type=F32)
        )
        gathered[place, s * depth:(s + 1) * depth, :] = total.astype(BF16)

    pl.semaphore_wait(barrier, surfs + 2)

    def ring_copy(direction, hops):
        if direction == 0:
            slot, to = (place + chips - hops) % chips, right
        else:
            slot, to = (place + hops) % chips, left
        return pltpu.make_async_remote_copy(
            src_ref=gathered.at[slot],
            dst_ref=gathered.at[slot],
            send_sem=ring_send.at[direction, hops],
            recv_sem=ring_recv.at[slot],
            device_id=(to, surf),
            device_id_type=MESH,
        )

    right_hops, left_hops = chips // 2, (chips - 1) // 2
    ring_copy(0, 0).start()
    ring_copy(1, 0).start()
    panel_copy = pltpu.make_async_remote_copy(
        src_ref=primaries_ref,
        dst_ref=partner,
        send_sem=panel_sems.at[0],
        recv_sem=panel_sems.at[1],
        device_id=(chip * 2 + 1 - core, surf),
        device_id_type=MESH,
    )
    panel_copy.start()

    block = 8

    def panel_spectra(source, which):
        def step(n, carry):
            rows = source[pl.ds(pl.multiple_of(n * block * width, block * width), block * width), :]
            value = jnp.dot(rows, forward_ref[:taps, :], preferred_element_type=F32)
            real, imag = value[:, :samples], value[:, samples:]
            first = lax.broadcasted_iota(jnp.int32, real.shape, 1) == 0
            shape = (block, width, 128)
            at = pl.ds(n * block, block)
            values = (
                jnp.where(first, 0.0, real),
                jnp.where(first, real, imag - real),
                jnp.where(first, imag, imag + real),
            )
            for ref, value in zip((e1, e2, e3), values):
                for f in range(samples // 128):
                    ref[f, at, which] = value[:, f * 128:(f + 1) * 128].reshape(shape)
            return carry

        lax.fori_loop(0, depth // block, step, 0)

    load_forward.wait()
    panel_spectra(primaries_ref, 0)
    panel_copy.wait_recv()
    panel_spectra(partner, 1)
    load_inverse.wait()

    def cross_copy(e, to):
        return pltpu.make_async_remote_copy(
            src_ref=crossing.at[e, to],
            dst_ref=crossed.at[e, surf],
            send_sem=cross_send.at[e, to],
            recv_sem=cross_recv.at[e, surf],
            device_id=(shot, to),
            device_id_type=MESH,
        )

    def leave_copy(slot):
        return pltpu.make_async_remote_copy(
            src_ref=leaving.at[slot],
            dst_ref=arrived.at[place],
            send_sem=leave_send.at[slot],
            recv_sem=leave_recv.at[place],
            device_id=(chip_at(slot, chips) * 2 + core, surf),
            device_id_type=MESH,
        )

    def slot_of(e):
        turn = (e + 1) % chips
        hops = (turn + 1) // 2
        return (place + chips + (1 - 2 * (turn % 2)) * hops) % chips

    def combined(e):
        for h in range(surfs):

            @pl.when(h != surf)
            def _():
                pltpu.make_async_copy(crossed.at[e, h], crossed.at[e, h], cross_recv.at[e, h]).wait()

        total = crossed[e, 0].astype(F32)
        for h in range(1, surfs):
            total = total + crossed[e, h].astype(F32)
        return total.astype(BF16)

    def pass_on(e):
        slot = slot_of(e)
        leaving[slot] = combined(e)
        leave_copy(slot).start()

    def one_chunk(e, carry):
        turn = (e + 1) % chips
        hops = (turn + 1) // 2

        @pl.when(turn % 2 == 1)
        def _():
            pltpu.make_async_copy(
                gathered.at[place], gathered.at[place], ring_recv.at[(place + chips - hops) % chips]
            ).wait()

            @pl.when(hops < right_hops)
            def _():
                ring_copy(0, hops).start()

            @pl.when(hops <= left_hops)
            def _():
                pltpu.make_async_copy(
                    gathered.at[place], gathered.at[place], ring_recv.at[(place + hops) % chips]
                ).wait()

            @pl.when(hops < left_hops)
            def _():
                ring_copy(1, hops).start()

        slot = slot_of(e)
        value = jnp.dot(gathered[slot], forward_ref[...], preferred_element_type=F32)
        real, imag = value[:, :samples], value[:, samples:]
        for k, part in enumerate((real + imag, real, imag)):
            for s in range(shots):
                for f in range(samples // 128):
                    factors[f, s * 3 + k, :depth, :] = part[
                        s * depth:(s + 1) * depth, f * 128:(f + 1) * 128
                    ]

        def one_tile(f, inner):
            lanes = pl.ds(pl.multiple_of(f * 128, 128), 128)
            tiles = 2 * width // 8

            def positions(n, sums):
                sums = list(sums)
                for j in range(UNROLL):
                    x = n * UNROLL + j
                    rows = [
                        [
                            jnp.broadcast_to(
                                factors.at[f, s * 3 + k, pl.ds(pl.multiple_of(n * UNROLL, UNROLL), UNROLL)][j:j + 1],
                                (8, 128),
                            )
                            for k in range(3)
                        ]
                        for s in range(shots)
                    ]
                    for t in range(tiles):
                        b, q = t * 8 // width, t * 8 % width
                        for k, ref in enumerate((e1, e2, e3)):
                            factor = ref[f, x, b, q:q + 8]
                            for s in range(shots):
                                at = (s * 3 + k) * tiles + t
                                sums[at] = sums[at] + factor * rows[s][k]
                return tuple(sums)

            zero = jnp.zeros((8, 128), F32)
            sums = lax.fori_loop(
                0, depth // UNROLL, positions, (zero,) * (3 * shots * tiles)
            )
            k1, k2, k3 = [
                [
                    jnp.concatenate(sums[(s * 3 + k) * tiles:(s * 3 + k + 1) * tiles], axis=0)
                    for s in range(shots)
                ]
                for k in range(3)
            ]
            first = lax.broadcasted_iota(jnp.int32, (2 * width, 128), 1) + f * 128 == 0
            imag_lanes = pl.ds(pl.multiple_of(samples + f * 128, 128), 128)
            for s in range(shots):
                re = jnp.where(first, k2[s], k1[s] - k3[s])
                im = jnp.where(first, k3[s], k1[s] + k2[s])
                for h in range(surfs):
                    for b in range(2):
                        low = ((h * shots + s) * 2 + b) * per_surf
                        src = b * width + h * per_surf
                        spectrum[low:low + per_surf, lanes] = re[src:src + per_surf]
                        spectrum[low:low + per_surf, imag_lanes] = im[src:src + per_surf]
            return inner

        lax.fori_loop(0, samples // 128, one_tile, 0)
        back = jnp.dot(spectrum[...].astype(BF16), inverse_ref[...], preferred_element_type=F32)
        rows = shots * 2 * per_surf
        for h in range(surfs):
            piece = back[h * rows:(h + 1) * rows].astype(BF16)

            @pl.when(surf == h)
            def _():
                crossed[e, h] = piece

            @pl.when(surf != h)
            def _():
                crossing[e, h] = piece
                cross_copy(e, h).start()

        @pl.when(e >= LAG)
        def _():
            pass_on(e - LAG)

        return carry

    lax.fori_loop(0, chips, one_chunk, 0)
    for e in range(chips - LAG, chips - 1):
        pass_on(e)
    arrived[place] = combined(chips - 1)

    first_panel, swap, base = where_ref[0:1, :], where_ref[1:2, :], where_ref[2:3, :]
    panel = first_panel + swap + core - 2 * core * swap
    target = base
    for n in range(panels):
        target = target + jnp.where(panel == n, plan_ref[n], 0)
    rows_out = data_ref.shape[0] * data_ref.shape[1]
    place_rows = jnp.where(
        lax.broadcasted_iota(jnp.int32, (rows_out, target.shape[1]), 0) == target, 1.0, 0.0
    ).astype(BF16)

    def settle(n, carry):
        for h in range(surfs):

            @pl.when(h != surf)
            def _():
                cross_copy(n, h).wait_send()

        @pl.when(n != place)
        def _():
            leave_copy(n).wait_send()
            pltpu.make_async_copy(arrived.at[n], arrived.at[n], leave_recv.at[n]).wait()

        return carry

    lax.fori_loop(0, chips, settle, 0)
    moved = arrived[...].reshape(target.shape[1], samples)
    prediction = jnp.dot(place_rows, moved, preferred_element_type=F32)
    receivers = data_ref.shape[1]
    for s in range(shots):
        out_ref[s] = data_ref[s] - scale_ref[s] * prediction[s * receivers:(s + 1) * receivers]

    for hops in range(right_hops):
        ring_copy(0, hops).wait_send()
    for hops in range(left_hops):
        ring_copy(1, hops).wait_send()
    panel_copy.wait_send()


def on_device(chips, surfs, data, positions, plan, primaries, scale):
    shots, receivers, samples = data.shape
    depth, width, _, taps = primaries.shape
    per_surf = width // surfs
    forward, inverse = fourier_matrices(samples)
    rows = shots * 2 * per_surf
    order = [
        (2 * chip_at(c, chips), b, (s * per_surf + q) * 2 * chips)
        for c in range(chips)
        for s in range(shots)
        for b in range(2)
        for q in range(per_surf)
    ]
    where_rows = np.zeros((8, len(order)), np.int32)
    where_rows[:3] = np.array(order, np.int32).T
    vmem = pl.BlockSpec(memory_space=pltpu.VMEM)
    smem = pl.BlockSpec(memory_space=pltpu.SMEM)
    sizes = (chips, surfs, shots, depth, width, samples, taps)
    return pl.pallas_call(
        functools.partial(kernel, sizes),
        out_shape=jax.ShapeDtypeStruct(data.shape, data.dtype),
        in_specs=[smem, smem] + [vmem] * 4 + [pl.BlockSpec(memory_space=pl.ANY)] * 2,
        out_specs=vmem,
        scratch_shapes=[
            pltpu.VMEM(forward.shape, BF16),
            pltpu.VMEM(inverse.shape, BF16),
            pltpu.VMEM((chips, shots * depth, samples), BF16),
            pltpu.VMEM((depth * width, taps), BF16),
            pltpu.VMEM((samples // 128, depth, 2, width, 128), F32),
            pltpu.VMEM((samples // 128, depth, 2, width, 128), F32),
            pltpu.VMEM((samples // 128, depth, 2, width, 128), F32),
            pltpu.VMEM((samples // 128, shots * 3, depth + 8, 128), F32),
            pltpu.VMEM((surfs * rows, 2 * samples), F32),
            pltpu.VMEM((chips, surfs, rows, samples), BF16),
            pltpu.VMEM((chips, surfs, rows, samples), BF16),
            pltpu.VMEM((chips, rows, samples), BF16),
            pltpu.VMEM((chips, rows, samples), BF16),
            pltpu.SemaphoreType.DMA((2,)),
            pltpu.SemaphoreType.DMA((2,)),
            pltpu.SemaphoreType.DMA((2, chips)),
            pltpu.SemaphoreType.DMA((chips,)),
            pltpu.SemaphoreType.DMA((chips, surfs)),
            pltpu.SemaphoreType.DMA((chips, surfs)),
            pltpu.SemaphoreType.DMA((chips,)),
            pltpu.SemaphoreType.DMA((chips,)),
        ],
        compiler_params=pltpu.CompilerParams(collective_id=0, has_side_effects=True),
        name="predict",
    )(
        plan,
        scale,
        jnp.asarray(where_rows),
        positions.reshape(1, receivers),
        data,
        primaries.reshape(depth * width, taps),
        jnp.asarray(forward),
        jnp.asarray(inverse),
    )


def solution(mesh):
    chips, surfs = mesh.shape["shot"] // 2, mesh.shape["surf"]
    in_specs = (P("shot", "surf", None), P("surf"), P(), P("surf", None, "shot", None), P("shot"))
    out_specs = P("shot", "surf", None)
    return jax.shard_map(
        functools.partial(on_device, chips, surfs),
        mesh=mesh, in_specs=in_specs, out_specs=out_specs, check_vma=False,
    )
```

profile of v0, /device:TPU:0, one launch (start us, length us, event | category | flops | bytes accessed | tf_op | source)
XLA Modules:
  0.0 32.3 jit_solution(2766139434834389730)
XLA Ops:
  0.0 30.4 %predict.1 = f32[2,128,512]{2,1,0:T(8,128)} custom-call(s32[16]{0:T(128)} %plan_ref.1, f32[2]{0:T(128)} %scale_ref.1, s32[8,256]{1,0:T(8,128)} %constant.6.clone.where_ref, s32[1,128]{1,0:T(1,128)} %bitcast.3, f32[2,128,512]{2,1,0:T(8,128)} %data_ref.1, bf16[512,256]{1,0:T(8,128)(2,1)} %bitcast.2, bf16[512,1024]{1,0:T(8,128)(2,1)} %constant.7.clone.forward_hbm, ...), custom_call_target="tpu_custom_call" | custom-call | tf_op jit(solution)/shard_map/predict/pallas_call | solution.py:359
  30.4 1.9 %copy.10 = f32[2,128,512]{2,1,0:T(8,128)} copy(f32[2,128,512]{2,1,0:T(8,128)} %predict.1) | data formatting | bytes 1048576
where the time goes:
time: 32.4 us; the launch traced here: 32.3 us
  Pallas kernels  30.4 us (94%)
  local copies, waits for them, and re-layouts  1.87 us (6%)
    pallas_call x1, Pallas kernels, on_device(): pl.pallas_call(functools.partial(kernel, sizes), out_shape=jax.ShapeDtype...  30.4 us
    unnamed x1, local copies, waits for them, and re-layouts  1.87 us

commit v1 on v0

v1 whole, which is shorter than its diff:
```python
import functools
import math

import jax
import jax.numpy as jnp
import ml_dtypes
import numpy as np
from jax import lax
from jax.experimental import pallas as pl
from jax.experimental.pallas import tpu as pltpu
from jax.sharding import PartitionSpec as P

MESH = pl.DeviceIdType.MESH
F32 = jnp.float32
BF16 = jnp.bfloat16
UNROLL = 16
LAG = 2
BLOCK = 8


def fourier_matrices(samples, length):
    half = length // 2
    time, frequency = np.arange(samples), np.arange(half)
    angles = (time[:, None] * frequency[None, :] % length) * (2.0 * math.pi / length)
    cosine, sine = np.cos(angles), np.sin(angles)
    forward_imag = -sine
    forward_imag[:, 0] = 1.0 - 2.0 * (time % 2)
    forward = np.concatenate([cosine, forward_imag], axis=1)
    weights = np.where(frequency == 0, 1.0, 2.0) / length
    weights = np.concatenate([weights, weights])
    inverse = forward.T * weights[:, None]
    return forward.astype(ml_dtypes.bfloat16), inverse.astype(ml_dtypes.bfloat16)


def predict_kernel(
    sizes,
    positions_hbm, data_hbm, primaries_hbm, forward_hbm, inverse_hbm,
    out_hbm,
    positions_ref, data_ref, forward_ref, inverse_ref, panels, gathered, e1, e2, e3, factors, spectrum,
    crossing, crossed, leaving,
    load_sems, data_sems, mate_sems, y_send, y_recv, relay_send, relay_recv, g_send, g_recv,
    cross_send, cross_recv, leave_send, leave_recv, own_sems,
):
    heights, surfs, shots, depth, width, samples, taps, half = sizes
    per_surf = width // surfs
    pieces = depth // BLOCK
    piece_rows = BLOCK * width
    items = 2 * heights
    tiles_f = half // 128
    shot = lax.axis_index("shot")
    surf = lax.axis_index("surf")
    core = shot % 2
    side = shot // 2 % 2
    height = shot // 4
    mate = (height * 2 + side) * 2 + 1 - core
    across = (height * 2 + 1 - side) * 2 + core

    def line(z):
        return (z * 2 + side) * 2 + core

    barrier = pltpu.get_barrier_semaphore()
    for to in (across, mate):
        pl.semaphore_signal(barrier, inc=1, device_id=(to, surf), device_id_type=MESH)
    for z in range(heights):

        @pl.when(z != height)
        def _():
            pl.semaphore_signal(barrier, inc=1, device_id=(line(z), surf), device_id_type=MESH)

    for h in range(surfs):

        @pl.when(h != surf)
        def _():
            pl.semaphore_signal(barrier, inc=1, device_id=(shot, h), device_id_type=MESH)

    load_positions = pltpu.make_async_copy(positions_hbm, positions_ref, load_sems.at[0])
    load_positions.start()
    load_data = [pltpu.make_async_copy(data_hbm.at[s], data_ref.at[s], data_sems.at[s]) for s in range(shots)]
    for load in load_data:
        load.start()
    load_panel = pltpu.make_async_copy(primaries_hbm, panels.at[0], load_sems.at[1])
    load_forward = pltpu.make_async_copy(forward_hbm, forward_ref, load_sems.at[2])
    load_inverse = pltpu.make_async_copy(inverse_hbm, inverse_ref, load_sems.at[3])
    load_panel.start()
    load_forward.start()
    load_inverse.start()

    pl.semaphore_wait(barrier, heights + surfs)

    mate_copy = pltpu.make_async_remote_copy(
        src_ref=primaries_hbm,
        dst_ref=panels.at[1],
        send_sem=mate_sems.at[0],
        recv_sem=mate_sems.at[1],
        device_id=(mate, surf),
        device_id_type=MESH,
    )

    def rows_of(n):
        return pl.ds(pl.multiple_of(n * piece_rows, piece_rows), piece_rows)

    def y_copy(n):
        return pltpu.make_async_remote_copy(
            src_ref=primaries_hbm.at[rows_of(n)],
            dst_ref=panels.at[2, rows_of(n)],
            send_sem=y_send.at[n],
            recv_sem=y_recv.at[n],
            device_id=(across, surf),
            device_id_type=MESH,
        )

    def relay_copy(n):
        return pltpu.make_async_remote_copy(
            src_ref=panels.at[2, rows_of(n)],
            dst_ref=panels.at[3, rows_of(n)],
            send_sem=relay_send.at[n],
            recv_sem=relay_recv.at[n],
            device_id=(mate, surf),
            device_id_type=MESH,
        )

    for n in range(pieces):
        y_copy(n).start()
    mate_copy.start()

    load_positions.wait()
    local = positions_ref[...] - surf * depth
    onehot = jnp.where(
        lax.broadcasted_iota(jnp.int32, (depth, local.shape[1]), 0) == local, 1.0, 0.0
    ).astype(BF16)
    for s in range(shots):
        load_data[s].wait()
        value = data_ref[s]
        top = value.astype(BF16)
        rest = value - top.astype(F32)
        middle = rest.astype(BF16)
        low = (rest - middle.astype(F32)).astype(BF16)
        total = (
            jnp.dot(onehot, top, preferred_element_type=F32)
            + jnp.dot(onehot, middle, preferred_element_type=F32)
            + jnp.dot(onehot, low, preferred_element_type=F32)
        )
        gathered[height, s * depth:(s + 1) * depth, :] = total.astype(BF16)

    def order(k):
        upper = height // (heights // 2)
        toward = 1 - 2 * upper
        short = height + upper * (heights - 1 - 2 * height)
        past = (k - 2 * short - 1 + 4 * heights) // (4 * heights)
        near = (k + 1) // 2 * (2 * (k % 2) - 1)
        return height + toward * (past * (k - short) + (1 - past) * near)

    def g_copy(z):
        return pltpu.make_async_remote_copy(
            src_ref=gathered.at[height],
            dst_ref=gathered.at[height],
            send_sem=g_send.at[z],
            recv_sem=g_recv.at[height],
            device_id=(line(z), surf),
            device_id_type=MESH,
        )

    for k in range(1, heights):
        g_copy(order(k)).start()

    def panel_spectra(which, pair, lane, n):
        rows = panels[which, rows_of(n), :]
        value = jnp.dot(rows, forward_ref[:taps, :], preferred_element_type=F32)
        real, imag = value[:, :half], value[:, half:]
        first = lax.broadcasted_iota(jnp.int32, real.shape, 1) == 0
        at = pl.ds(pl.multiple_of(n * BLOCK, BLOCK), BLOCK)
        values = (
            jnp.where(first, 0.0, real),
            jnp.where(first, real, imag - real),
            jnp.where(first, imag, imag + real),
        )
        for ref, value in zip((e1, e2, e3), values):
            for f in range(tiles_f):
                ref[pair, f, at, lane] = value[:, f * 128:(f + 1) * 128].reshape(BLOCK, width, 128)

    def whole_panel(which, pair, lane):
        def step(n, carry):
            panel_spectra(which, pair, lane, n)
            return carry

        lax.fori_loop(0, pieces, step, 0)

    load_forward.wait()
    load_panel.wait()
    whole_panel(0, 0, 0)
    mate_copy.wait_recv()
    whole_panel(1, 0, 1)
    load_inverse.wait()

    def cross_copy(e, to):
        return pltpu.make_async_remote_copy(
            src_ref=crossing.at[e, to],
            dst_ref=crossed.at[e, surf],
            send_sem=cross_send.at[e, to],
            recv_sem=cross_recv.at[e, surf],
            device_id=(shot, to),
            device_id_type=MESH,
        )

    def place_of(e):
        pair = e // heights
        return pair, e + pair * (items - 1 - 2 * e)

    def leave_copy(e):
        pair, k = place_of(e)
        return pltpu.make_async_remote_copy(
            src_ref=leaving.at[e],
            dst_ref=out_hbm.at[height, pair],
            send_sem=leave_send.at[e],
            recv_sem=leave_recv.at[height, pair],
            device_id=(line(order(k)), surf),
            device_id_type=MESH,
        )

    def own_copy(e):
        pair, _ = place_of(e)
        return pltpu.make_async_copy(leaving.at[e], out_hbm.at[height, pair], own_sems.at[pair])

    def pass_on(e):
        for h in range(surfs):

            @pl.when(h != surf)
            def _():
                pltpu.make_async_copy(crossed.at[e, h], crossed.at[e, h], cross_recv.at[e, h]).wait()

        total = crossed[e, 0].astype(F32)
        for h in range(1, surfs):
            total = total + crossed[e, h].astype(F32)
        leaving[e] = total.astype(BF16)
        _, k = place_of(e)

        @pl.when(k != 0)
        def _():
            leave_copy(e).start()

        @pl.when(k == 0)
        def _():
            own_copy(e).start()

    def shot_spectra(k):
        slot = order(k)

        @pl.when(k != 0)
        def _():
            pltpu.make_async_copy(gathered.at[slot], gathered.at[slot], g_recv.at[slot]).wait()

        value = jnp.dot(gathered[slot], forward_ref[...], preferred_element_type=F32)
        real, imag = value[:, :half], value[:, half:]
        for m, part in enumerate((real + imag, real, imag)):
            for s in range(shots):
                for f in range(tiles_f):
                    factors[k, f, s * 3 + m, :depth, :] = part[
                        s * depth:(s + 1) * depth, f * 128:(f + 1) * 128
                    ]

    def work(e, k, pair):
        def one_tile(f, inner):
            lanes = pl.ds(pl.multiple_of(f * 128, 128), 128)
            tiles = 2 * width // 8

            def positions(n, sums):
                sums = list(sums)
                for j in range(UNROLL):
                    x = n * UNROLL + j
                    rows = [
                        [
                            jnp.broadcast_to(
                                factors.at[k, f, s * 3 + m, pl.ds(pl.multiple_of(n * UNROLL, UNROLL), UNROLL)][j:j + 1],
                                (8, 128),
                            )
                            for m in range(3)
                        ]
                        for s in range(shots)
                    ]
                    for t in range(tiles):
                        b, q = t * 8 // width, t * 8 % width
                        for m, ref in enumerate((e1, e2, e3)):
                            factor = ref[pair, f, x, b, q:q + 8]
                            for s in range(shots):
                                at = (s * 3 + m) * tiles + t
                                sums[at] = sums[at] + factor * rows[s][m]
                return tuple(sums)

            zero = jnp.zeros((8, 128), F32)
            sums = lax.fori_loop(
                0, depth // UNROLL, positions, (zero,) * (3 * shots * tiles)
            )
            k1, k2, k3 = [
                [
                    jnp.concatenate(sums[(s * 3 + m) * tiles:(s * 3 + m + 1) * tiles], axis=0)
                    for s in range(shots)
                ]
                for m in range(3)
            ]
            first = lax.broadcasted_iota(jnp.int32, (2 * width, 128), 1) + f * 128 == 0
            imag_lanes = pl.ds(pl.multiple_of(half + f * 128, 128), 128)
            for s in range(shots):
                re = jnp.where(first, k2[s], k1[s] - k3[s])
                im = jnp.where(first, k3[s], k1[s] + k2[s])
                for h in range(surfs):
                    for b in range(2):
                        low = ((h * shots + s) * 2 + b) * per_surf
                        src = b * width + h * per_surf
                        spectrum[low:low + per_surf, lanes] = re[src:src + per_surf]
                        spectrum[low:low + per_surf, imag_lanes] = im[src:src + per_surf]
            return inner

        lax.fori_loop(0, tiles_f, one_tile, 0)
        back = jnp.dot(spectrum[...].astype(BF16), inverse_ref[...], preferred_element_type=F32)
        rows = shots * 2 * per_surf
        for h in range(surfs):
            piece = back[h * rows:(h + 1) * rows].astype(BF16)

            @pl.when(surf == h)
            def _():
                crossed[e, h] = piece

            @pl.when(surf != h)
            def _():
                crossing[e, h] = piece
                cross_copy(e, h).start()

    def take_piece(n):
        pltpu.make_async_copy(panels.at[2, rows_of(n)], panels.at[2, rows_of(n)], y_recv.at[n]).wait()
        relay_copy(n).start()
        panel_spectra(2, 1, 0, n)

    early = min(heights - 1, pieces)

    def first_pair(e, carry):
        @pl.when(e * (early + 1 - e) > 0)
        def _():
            take_piece(e - 1)

        shot_spectra(e)
        work(e, e, 0)

        @pl.when(e >= LAG)
        def _():
            pass_on(e - LAG)

        return carry

    lax.fori_loop(0, heights, first_pair, 0)

    def late_piece(n, carry):
        take_piece(n)
        return carry

    lax.fori_loop(early, pieces, late_piece, 0)

    def relayed_piece(n, carry):
        pltpu.make_async_copy(panels.at[3, rows_of(n)], panels.at[3, rows_of(n)], relay_recv.at[n]).wait()
        panel_spectra(3, 1, 1, n)
        return carry

    lax.fori_loop(0, pieces, relayed_piece, 0)

    def second_pair(e, carry):
        pass_on(e - LAG)
        work(e, items - 1 - e, 1)
        return carry

    lax.fori_loop(heights, items, second_pair, 0)
    for e in range(items - LAG, items):
        pass_on(e)

    def settle(z, carry):
        for pair in range(2):
            at = pair * (items - 1)

            @pl.when(z != height)
            def _():
                pltpu.make_async_copy(out_hbm.at[z, pair], out_hbm.at[z, pair], leave_recv.at[z, pair]).wait()

        @pl.when(z != height)
        def _():
            g_copy(z).wait_send()

        @pl.when(z != 0)
        def _():
            leave_copy(z).wait_send()
            leave_copy(items - 1 - z).wait_send()

        return carry

    lax.fori_loop(0, heights, settle, 0)
    own_copy(0).wait()
    own_copy(items - 1).wait()

    def settle_cross(e, carry):
        for h in range(surfs):

            @pl.when(h != surf)
            def _():
                cross_copy(e, h).wait_send()

        return carry

    lax.fori_loop(0, items, settle_cross, 0)
    for n in range(pieces):
        y_copy(n).wait_send()
        relay_copy(n).wait_send()
    mate_copy.wait_send()


def subtract_kernel(panels, plan_ref, scale_ref, where_ref, data_ref, moved_ref, out_ref):
    shot = lax.axis_index("shot")
    core = shot % 2
    side = shot // 2 % 2
    s = pl.program_id(0)
    line, far, swap, base = [where_ref[n:n + 1, :] for n in range(4)]
    panel = line + 2 * (far + side - 2 * side * far) + swap + core - 2 * core * swap
    target = base
    for n in range(panels):
        target = target + jnp.where(panel == n, plan_ref[n], 0)
    receivers = data_ref.shape[1]
    place_rows = jnp.where(
        lax.broadcasted_iota(jnp.int32, (receivers, target.shape[1]), 0) + s * receivers == target, 1.0, 0.0
    ).astype(BF16)
    prediction = jnp.dot(place_rows, moved_ref[...], preferred_element_type=F32)
    out_ref[0] = data_ref[0] - scale_ref[s] * prediction


def on_device(heights, surfs, data, positions, plan, primaries, scale):
    shots, receivers, samples = data.shape
    depth, width, _, taps = primaries.shape
    per_surf = width // surfs
    half = -(-(samples + taps - 1) // 256) * 128
    forward, inverse = fourier_matrices(samples, 2 * half)
    rows = shots * 2 * per_surf
    items = 2 * heights
    pieces = depth // BLOCK
    panels = 4 * heights
    order = [
        (4 * z, pair, b, s * receivers + q * panels)
        for z in range(heights)
        for pair in range(2)
        for s in range(shots)
        for b in range(2)
        for q in range(per_surf)
    ]
    where_rows = np.zeros((8, len(order)), np.int32)
    where_rows[:4] = np.array(order, np.int32).T
    anywhere = pl.BlockSpec(memory_space=pl.ANY)
    dma = pltpu.SemaphoreType.DMA
    sizes = (heights, surfs, shots, depth, width, samples, taps, half)
    spectra = pltpu.VMEM((2, half // 128, depth, 2, width, 128), F32)
    moved = pl.pallas_call(
        functools.partial(predict_kernel, sizes),
        out_shape=jax.ShapeDtypeStruct((heights, 2, rows, samples), BF16),
        in_specs=[anywhere] * 5,
        out_specs=anywhere,
        scratch_shapes=[
            pltpu.VMEM((1, receivers), jnp.int32),
            pltpu.VMEM(data.shape, F32),
            pltpu.VMEM(forward.shape, BF16),
            pltpu.VMEM(inverse.shape, BF16),
            pltpu.VMEM((4, depth * width, taps), BF16),
            pltpu.VMEM((heights, shots * depth, samples), BF16),
            spectra,
            spectra,
            spectra,
            pltpu.VMEM((heights, half // 128, shots * 3, depth + 8, 128), F32),
            pltpu.VMEM((surfs * rows, 2 * half), F32),
            pltpu.VMEM((items, surfs, rows, samples), BF16),
            pltpu.VMEM((items, surfs, rows, samples), BF16),
            pltpu.VMEM((items, rows, samples), BF16),
            dma((4,)),
            dma((shots,)),
            dma((2,)),
            dma((pieces,)),
            dma((pieces,)),
            dma((pieces,)),
            dma((pieces,)),
            dma((heights,)),
            dma((heights,)),
            dma((items, surfs)),
            dma((items, surfs)),
            dma((items,)),
            dma((heights, 2)),
            dma((2,)),
        ],
        compiler_params=pltpu.CompilerParams(collective_id=0, has_side_effects=True),
        name="predict",
    )(
        positions.reshape(1, receivers),
        data,
        primaries.reshape(depth * width, taps),
        jnp.asarray(forward),
        jnp.asarray(inverse),
    )
    smem = pl.BlockSpec(memory_space=pltpu.SMEM)
    traces = pl.BlockSpec((1, receivers, samples), lambda s: (s, 0, 0))
    return pl.pallas_call(
        functools.partial(subtract_kernel, panels),
        out_shape=jax.ShapeDtypeStruct(data.shape, data.dtype),
        grid=(shots,),
        in_specs=[
            smem,
            smem,
            pl.BlockSpec(where_rows.shape, lambda s: (0, 0)),
            traces,
            pl.BlockSpec((len(order), samples), lambda s: (0, 0)),
        ],
        out_specs=traces,
        name="subtract",
    )(plan, scale, jnp.asarray(where_rows), data, moved.reshape(len(order), samples))


def solution(mesh):
    heights, surfs = mesh.shape["shot"] // 4, mesh.shape["surf"]
    in_specs = (P("shot", "surf", None), P("surf"), P(), P("surf", None, "shot", None), P("shot"))
    out_specs = P("shot", "surf", None)
    return jax.shard_map(
        functools.partial(on_device, heights, surfs),
        mesh=mesh, in_specs=in_specs, out_specs=out_specs, check_vma=False,
    )
```

time: 32.4 us -> 29.9 us (0.923)
  local copies, waits for them, and re-layouts: 1.87 us -> 0 us
  Pallas kernels: 30.4 us -> 29.7 us
    unnamed x1 -> x0, local copies, waits for them, and re-layouts: 1.87 us -> none
    pallas_call x1 -> x2, Pallas kernels: 30.4 us -> 29.7 us  [the longest x1 27.5 us: on_device(): pl.pallas_call(functools.partial(predict_kernel, sizes), out_shape=jax.Sh...]
where the time goes in v1:
time: 29.9 us; the launch traced here: 29.7 us
  Pallas kernels  29.7 us (99%)
    pallas_call x1, Pallas kernels, on_device(): pl.pallas_call(functools.partial(predict_kernel, sizes), out_shape=jax.Sh...  27.5 us
    pallas_call x1, Pallas kernels, on_device(): pl.pallas_call(functools.partial(subtract_kernel, panels), out_shape=jax....  2.23 us

profile of v1, /device:TPU:0, one launch (start us, length us, event | category | flops | bytes accessed | tf_op | source)
XLA Modules:
  0.0 29.7 jit_solution(12937083291156809122)
XLA Ops:
  0.0 27.5 %predict.1 = bf16[4,2,32,512]{3,2,1,0:T(8,128)(2,1)} custom-call(s32[1,128]{1,0:T(1,128)} %bitcast.5, f32[2,128,512]{2,1,0:T(8,128)} %data_ref.1, bf16[512,256]{1,0:T(8,128)(2,1)} %bitcast.4, bf16[512,768]{1,0:T(8,128)(2,1)} %constant.6.clone.forward_hbm, bf16[768,512]{1,0:T(8,128)(2,1)} %constant.7.clone.inverse_hbm), custom_call_target="tpu_custom_call" | custom-call | tf_op jit(solution)/shard_map/predict/pallas_call | solution.py:454
  27.5 2.2 %subtract.1 = f32[2,128,512]{2,1,0:T(8,128)} custom-call(s32[16]{0:T(128)} %plan_ref.1, f32[2]{0:T(128)} %scale_ref.1, s32[8,256]{1,0:T(8,128)} %constant.8.clone.where_ref, f32[2,128,512]{2,1,0:T(8,128)} %data_ref.1, bf16[256,512]{1,0:T(8,128)(2,1)} %bitcast.3), custom_call_target="tpu_custom_call" | custom-call | tf_op jit(solution)/shard_map/subtract/pallas_call | solution.py:500

commit v2 on v1

--- a/solution.py
+++ b/solution.py
@@ -14,8 +14,7 @@
 F32 = jnp.float32
 BF16 = jnp.bfloat16
 UNROLL = 16
-LAG = 2
-BLOCK = 8
+BLOCK = 16
 
 
 def fourier_matrices(samples, length):
@@ -34,17 +33,18 @@
 
 def predict_kernel(
     sizes,
-    positions_hbm, data_hbm, primaries_hbm, forward_hbm, inverse_hbm,
-    out_hbm,
-    positions_ref, data_ref, forward_ref, inverse_ref, panels, gathered, e1, e2, e3, factors, spectrum,
-    crossing, crossed, leaving,
+    plan_hbm, scale_hbm, where_hbm, positions_hbm, data_hbm, primaries_hbm, forward_hbm, inverse_hbm,
+    out_ref,
+    plan_ref, scale_ref, where_ref, positions_ref, data_ref, forward_ref, inverse_ref,
+    panels, gathered, e1, e2, e3, factors, spectrum, leaving, arrived, place_rows, prediction,
     load_sems, data_sems, mate_sems, y_send, y_recv, relay_send, relay_recv, g_send, g_recv,
-    cross_send, cross_recv, leave_send, leave_recv, own_sems,
+    leave_send, leave_recv, own_sems,
 ):
     heights, surfs, shots, depth, width, samples, taps, half = sizes
     per_surf = width // surfs
     pieces = depth // BLOCK
     piece_rows = BLOCK * width
+    rows_item = shots * 2 * per_surf
     items = 2 * heights
     tiles_f = half // 128
     shot = lax.axis_index("shot")
@@ -62,16 +62,11 @@
     for to in (across, mate):
         pl.semaphore_signal(barrier, inc=1, device_id=(to, surf), device_id_type=MESH)
     for z in range(heights):
-
-        @pl.when(z != height)
-        def _():
-            pl.semaphore_signal(barrier, inc=1, device_id=(line(z), surf), device_id_type=MESH)
-
-    for h in range(surfs):
-
-        @pl.when(h != surf)
-        def _():
-            pl.semaphore_signal(barrier, inc=1, device_id=(shot, h), device_id_type=MESH)
+        for h in range(surfs):
+
+            @pl.when((z != height) | (h != surf))
+            def _():
+                pl.semaphore_signal(barrier, inc=1, device_id=(line(z), h), device_id_type=MESH)
 
     load_positions = pltpu.make_async_copy(positions_hbm, positions_ref, load_sems.at[0])
     load_positions.start()
@@ -81,12 +76,10 @@
     load_panel = pltpu.make_async_copy(primaries_hbm, panels.at[0], load_sems.at[1])
     load_forward = pltpu.make_async_copy(forward_hbm, forward_ref, load_sems.at[2])
     load_inverse = pltpu.make_async_copy(inverse_hbm, inverse_ref, load_sems.at[3])
-    load_panel.start()
-    load_forward.start()
-    load_inverse.start()
-
-    pl.semaphore_wait(barrier, heights + surfs)
-
+    load_small = [
+        pltpu.make_async_copy(src, dst, load_sems.at[4 + n])
+        for n, (src, dst) in enumerate(((plan_hbm, plan_ref), (scale_hbm, scale_ref), (where_hbm, where_ref)))
+    ]
     mate_copy = pltpu.make_async_remote_copy(
         src_ref=primaries_hbm,
         dst_ref=panels.at[1],
@@ -119,10 +112,6 @@
             device_id_type=MESH,
         )
 
-    for n in range(pieces):
-        y_copy(n).start()
-    mate_copy.start()
-
     load_positions.wait()
     local = positions_ref[...] - surf * depth
     onehot = jnp.where(
@@ -130,6 +119,12 @@
     ).astype(BF16)
     for s in range(shots):
         load_data[s].wait()
+        if s == shots - 1:
+            load_panel.start()
+            load_forward.start()
+            load_inverse.start()
+            for load in load_small:
+                load.start()
         value = data_ref[s]
         top = value.astype(BF16)
         rest = value - top.astype(F32)
@@ -160,15 +155,12 @@
             device_id_type=MESH,
         )
 
-    for k in range(1, heights):
-        g_copy(order(k)).start()
-
-    def panel_spectra(which, pair, lane, n):
-        rows = panels[which, rows_of(n), :]
+    def panel_spectra(which, pair, lane, n, block):
+        rows = panels[which, pl.ds(pl.multiple_of(n * block * width, block * width), block * width), :]
         value = jnp.dot(rows, forward_ref[:taps, :], preferred_element_type=F32)
         real, imag = value[:, :half], value[:, half:]
         first = lax.broadcasted_iota(jnp.int32, real.shape, 1) == 0
-        at = pl.ds(pl.multiple_of(n * BLOCK, BLOCK), BLOCK)
+        at = pl.ds(pl.multiple_of(n * block, block), block)
         values = (
             jnp.where(first, 0.0, real),
             jnp.where(first, real, imag - real),
@@ -176,79 +168,30 @@
         )
         for ref, value in zip((e1, e2, e3), values):
             for f in range(tiles_f):
-                ref[pair, f, at, lane] = value[:, f * 128:(f + 1) * 128].reshape(BLOCK, width, 128)
-
-    def whole_panel(which, pair, lane):
-        def step(n, carry):
-            panel_spectra(which, pair, lane, n)
-            return carry
-
-        lax.fori_loop(0, pieces, step, 0)
-
-    load_forward.wait()
-    load_panel.wait()
-    whole_panel(0, 0, 0)
-    mate_copy.wait_recv()
-    whole_panel(1, 0, 1)
-    load_inverse.wait()
-
-    def cross_copy(e, to):
-        return pltpu.make_async_remote_copy(
-            src_ref=crossing.at[e, to],
-            dst_ref=crossed.at[e, surf],
-            send_sem=cross_send.at[e, to],
-            recv_sem=cross_recv.at[e, surf],
-            device_id=(shot, to),
-            device_id_type=MESH,
-        )
+                ref[pair, f, at, lane] = value[:, f * 128:(f + 1) * 128].reshape(block, width, 128)
 
     def place_of(e):
         pair = e // heights
         return pair, e + pair * (items - 1 - 2 * e)
 
-    def leave_copy(e):
+    def leave_copy(e, h):
         pair, k = place_of(e)
         return pltpu.make_async_remote_copy(
-            src_ref=leaving.at[e],
-            dst_ref=out_hbm.at[height, pair],
-            send_sem=leave_send.at[e],
-            recv_sem=leave_recv.at[height, pair],
-            device_id=(line(order(k)), surf),
+            src_ref=leaving.at[e, h],
+            dst_ref=arrived.at[height, pair, surf],
+            send_sem=leave_send.at[e, h],
+            recv_sem=leave_recv.at[height, pair, surf],
+            device_id=(line(order(k)), h),
             device_id_type=MESH,
         )
 
-    def own_copy(e):
-        pair, _ = place_of(e)
-        return pltpu.make_async_copy(leaving.at[e], out_hbm.at[height, pair], own_sems.at[pair])
-
-    def pass_on(e):
-        for h in range(surfs):
-
-            @pl.when(h != surf)
-            def _():
-                pltpu.make_async_copy(crossed.at[e, h], crossed.at[e, h], cross_recv.at[e, h]).wait()
-
-        total = crossed[e, 0].astype(F32)
-        for h in range(1, surfs):
-            total = total + crossed[e, h].astype(F32)
-        leaving[e] = total.astype(BF16)
-        _, k = place_of(e)
-
-        @pl.when(k != 0)
-        def _():
-            leave_copy(e).start()
-
-        @pl.when(k == 0)
-        def _():
-            own_copy(e).start()
+    def own_copy(pair):
+        return pltpu.make_async_copy(
+            leaving.at[pair * (items - 1), surf], arrived.at[height, pair, surf], own_sems.at[pair]
+        )
 
     def shot_spectra(k):
         slot = order(k)
-
-        @pl.when(k != 0)
-        def _():
-            pltpu.make_async_copy(gathered.at[slot], gathered.at[slot], g_recv.at[slot]).wait()
-
         value = jnp.dot(gathered[slot], forward_ref[...], preferred_element_type=F32)
         real, imag = value[:, :half], value[:, half:]
         for m, part in enumerate((real + imag, real, imag)):
@@ -314,117 +257,131 @@
         back = jnp.dot(spectrum[...].astype(BF16), inverse_ref[...], preferred_element_type=F32)
         rows = shots * 2 * per_surf
         for h in range(surfs):
-            piece = back[h * rows:(h + 1) * rows].astype(BF16)
-
-            @pl.when(surf == h)
+            leaving[e, h] = back[h * rows:(h + 1) * rows].astype(BF16)
+        for h in range(surfs):
+
+            @pl.when((k != 0) | (h != surf))
             def _():
-                crossed[e, h] = piece
-
-            @pl.when(surf != h)
-            def _():
-                crossing[e, h] = piece
-                cross_copy(e, h).start()
+                leave_copy(e, h).start()
+
+        @pl.when(k == 0)
+        def _():
+            own_copy(pair).start()
+
+    pl.semaphore_wait(barrier, heights * surfs + 1)
+    mate_copy.start()
+    for k in range(1, heights):
+        g_copy(order(k)).start()
+    for n in range(pieces):
+        y_copy(n).start()
+
+    load_forward.wait()
+    load_panel.wait()
+    panel_spectra(0, 0, 0, 0, depth)
+    shot_spectra(0)
+    for load in load_small:
+        load.wait()
+    line_row, far, swap, base = [where_ref[n:n + 1, :] for n in range(4)]
+    panel = line_row + 2 * (far + side - 2 * side * far) + swap + core - 2 * core * swap
+    target = base
+    for n in range(4 * heights):
+        target = target + jnp.where(panel == n, plan_ref[n], 0)
+    place_rows[...] = jnp.where(
+        lax.broadcasted_iota(jnp.int32, place_rows.shape, 0) == target, 1.0, 0.0
+    ).astype(BF16)
+    load_inverse.wait()
+    mate_copy.wait_recv()
+    panel_spectra(1, 0, 1, 0, depth)
 
     def take_piece(n):
         pltpu.make_async_copy(panels.at[2, rows_of(n)], panels.at[2, rows_of(n)], y_recv.at[n]).wait()
         relay_copy(n).start()
-        panel_spectra(2, 1, 0, n)
-
-    early = min(heights - 1, pieces)
+        panel_spectra(2, 1, 0, n, BLOCK)
+
+    work(0, 0, 0)
 
     def first_pair(e, carry):
-        @pl.when(e * (early + 1 - e) > 0)
-        def _():
-            take_piece(e - 1)
-
+        slot = order(e)
+        pltpu.make_async_copy(gathered.at[slot], gathered.at[slot], g_recv.at[slot]).wait()
         shot_spectra(e)
         work(e, e, 0)
-
-        @pl.when(e >= LAG)
-        def _():
-            pass_on(e - LAG)
-
         return carry
 
-    lax.fori_loop(0, heights, first_pair, 0)
-
-    def late_piece(n, carry):
+    def y_piece(n, carry):
         take_piece(n)
         return carry
 
-    lax.fori_loop(early, pieces, late_piece, 0)
+    first_pair(1, 0)
+    y_piece(0, 0)
+    lax.fori_loop(2, heights, first_pair, 0)
+    lax.fori_loop(1, pieces, y_piece, 0)
 
     def relayed_piece(n, carry):
         pltpu.make_async_copy(panels.at[3, rows_of(n)], panels.at[3, rows_of(n)], relay_recv.at[n]).wait()
-        panel_spectra(3, 1, 1, n)
+        panel_spectra(3, 1, 1, n, BLOCK)
         return carry
 
     lax.fori_loop(0, pieces, relayed_piece, 0)
 
     def second_pair(e, carry):
-        pass_on(e - LAG)
         work(e, items - 1 - e, 1)
         return carry
 
     lax.fori_loop(heights, items, second_pair, 0)
-    for e in range(items - LAG, items):
-        pass_on(e)
+
+    chunk = 2 * surfs * rows_item
+    receivers = data_ref.shape[1]
+    for k in reversed(range(heights)):
+        z = order(k)
+        for pair in range(2):
+            for h in range(surfs):
+                slot = arrived.at[z, pair, h]
+                if k:
+                    pltpu.make_async_copy(slot, slot, leave_recv.at[z, pair, h]).wait()
+                else:
+
+                    @pl.when(h != surf)
+                    def _():
+                        pltpu.make_async_copy(slot, slot, leave_recv.at[z, pair, h]).wait()
+
+                    @pl.when(h == surf)
+                    def _():
+                        own_copy(pair).wait()
+
+        part = jnp.dot(
+            place_rows[:, pl.ds(pl.multiple_of(z * chunk, chunk), chunk)],
+            arrived[z].reshape(chunk, samples),
+            preferred_element_type=F32,
+        )
+        if k == heights - 1:
+            prediction[...] = part
+        elif k:
+            prediction[...] += part
+        else:
+            for s in range(shots):
+                low = s * receivers
+                total = prediction[low:low + receivers] + part[low:low + receivers]
+                out_ref[s] = data_ref[s] - scale_ref[s] * total
 
     def settle(z, carry):
-        for pair in range(2):
-            at = pair * (items - 1)
-
-            @pl.when(z != height)
+        for h in range(surfs):
+
+            @pl.when((z != 0) | (h != surf))
             def _():
-                pltpu.make_async_copy(out_hbm.at[z, pair], out_hbm.at[z, pair], leave_recv.at[z, pair]).wait()
+                leave_copy(z, h).wait_send()
+                leave_copy(items - 1 - z, h).wait_send()
 
         @pl.when(z != height)
         def _():
             g_copy(z).wait_send()
 
-        @pl.when(z != 0)
-        def _():
-            leave_copy(z).wait_send()
-            leave_copy(items - 1 - z).wait_send()
-
         return carry
 
     lax.fori_loop(0, heights, settle, 0)
-    own_copy(0).wait()
-    own_copy(items - 1).wait()
-
-    def settle_cross(e, carry):
-        for h in range(surfs):
-
-            @pl.when(h != surf)
-            def _():
-                cross_copy(e, h).wait_send()
-
-        return carry
-
-    lax.fori_loop(0, items, settle_cross, 0)
     for n in range(pieces):
         y_copy(n).wait_send()
         relay_copy(n).wait_send()
     mate_copy.wait_send()
-
-
-def subtract_kernel(panels, plan_ref, scale_ref, where_ref, data_ref, moved_ref, out_ref):
-    shot = lax.axis_index("shot")
-    core = shot % 2
-    side = shot // 2 % 2
-    s = pl.program_id(0)
-    line, far, swap, base = [where_ref[n:n + 1, :] for n in range(4)]
-    panel = line + 2 * (far + side - 2 * side * far) + swap + core - 2 * core * swap
-    target = base
-    for n in range(panels):
-        target = target + jnp.where(panel == n, plan_ref[n], 0)
-    receivers = data_ref.shape[1]
-    place_rows = jnp.where(
-        lax.broadcasted_iota(jnp.int32, (receivers, target.shape[1]), 0) + s * receivers == target, 1.0, 0.0
-    ).astype(BF16)
-    prediction = jnp.dot(place_rows, moved_ref[...], preferred_element_type=F32)
-    out_ref[0] = data_ref[0] - scale_ref[s] * prediction
 
 
 def on_device(heights, surfs, data, positions, plan, primaries, scale):
@@ -441,6 +398,7 @@
         (4 * z, pair, b, s * receivers + q * panels)
         for z in range(heights)
         for pair in range(2)
+        for _ in range(surfs)
         for s in range(shots)
         for b in range(2)
         for q in range(per_surf)
@@ -451,12 +409,15 @@
     dma = pltpu.SemaphoreType.DMA
     sizes = (heights, surfs, shots, depth, width, samples, taps, half)
     spectra = pltpu.VMEM((2, half // 128, depth, 2, width, 128), F32)
-    moved = pl.pallas_call(
+    return pl.pallas_call(
         functools.partial(predict_kernel, sizes),
-        out_shape=jax.ShapeDtypeStruct((heights, 2, rows, samples), BF16),
-        in_specs=[anywhere] * 5,
-        out_specs=anywhere,
+        out_shape=pltpu.VMEM(data.shape, F32),
+        in_specs=[anywhere] * 8,
+        out_specs=pl.BlockSpec(memory_space=pltpu.VMEM),
         scratch_shapes=[
+            pltpu.SMEM(plan.shape, jnp.int32),
+            pltpu.SMEM(scale.shape, F32),
+            pltpu.VMEM(where_rows.shape, jnp.int32),
             pltpu.VMEM((1, receivers), jnp.int32),
             pltpu.VMEM(data.shape, F32),
             pltpu.VMEM(forward.shape, BF16),
@@ -469,9 +430,10 @@
             pltpu.VMEM((heights, half // 128, shots * 3, depth + 8, 128), F32),
             pltpu.VMEM((surfs * rows, 2 * half), F32),
             pltpu.VMEM((items, surfs, rows, samples), BF16),
-            pltpu.VMEM((items, surfs, rows, samples), BF16),
-            pltpu.VMEM((items, rows, samples), BF16),
-            dma((4,)),
+            pltpu.VMEM((heights, 2, surfs, rows, samples), BF16),
+            pltpu.VMEM((shots * receivers, len(order)), BF16),
+            pltpu.VMEM((shots * receivers, samples), F32),
+            dma((7,)),
             dma((shots,)),
             dma((2,)),
             dma((pieces,)),
@@ -481,36 +443,23 @@
             dma((heights,)),
             dma((heights,)),
             dma((items, surfs)),
-            dma((items, surfs)),
-            dma((items,)),
-            dma((heights, 2)),
+            dma((heights, 2, surfs)),
             dma((2,)),
         ],
-        compiler_params=pltpu.CompilerParams(collective_id=0, has_side_effects=True),
+        compiler_params=pltpu.CompilerParams(
+            collective_id=0, has_side_effects=True, vmem_limit_bytes=57000 * 1024
+        ),
         name="predict",
     )(
+        plan,
+        scale,
+        jnp.asarray(where_rows),
         positions.reshape(1, receivers),
         data,
         primaries.reshape(depth * width, taps),
         jnp.asarray(forward),
         jnp.asarray(inverse),
     )
-    smem = pl.BlockSpec(memory_space=pltpu.SMEM)
-    traces = pl.BlockSpec((1, receivers, samples), lambda s: (s, 0, 0))
-    return pl.pallas_call(
-        functools.partial(subtract_kernel, panels),
-        out_shape=jax.ShapeDtypeStruct(data.shape, data.dtype),
-        grid=(shots,),
-        in_specs=[
-            smem,
-            smem,
-            pl.BlockSpec(where_rows.shape, lambda s: (0, 0)),
-            traces,
-            pl.BlockSpec((len(order), samples), lambda s: (0, 0)),
-        ],
-        out_specs=traces,
-        name="subtract",
-    )(plan, scale, jnp.asarray(where_rows), data, moved.reshape(len(order), samples))
 
 
 def solution(mesh):

time: 29.9 us -> 25.2 us (0.84)
  Pallas kernels: 29.7 us -> 24.3 us
  local copies, waits for them, and re-layouts: 0 us -> 0.8 us
    pallas_call x2 -> x1, Pallas kernels: 29.7 us -> 24.3 us  [on_device(): pl.pallas_call(functools.partial(predict_kernel, sizes), out_shape=pltpu....]
    unnamed x0 -> x1, local copies, waits for them, and re-layouts: none -> 0.8 us
where the time goes in v2:
time: 25.2 us; the launch traced here: 25.1 us
  Pallas kernels  24.3 us (96%)
  local copies, waits for them, and re-layouts  0.8 us (3%)
    pallas_call x1, Pallas kernels, on_device(): pl.pallas_call(functools.partial(predict_kernel, sizes), out_shape=pltpu....  24.3 us
    unnamed x1, local copies, waits for them, and re-layouts  0.8 us

profile of v2, /device:TPU:0, one launch (start us, length us, event | category | flops | bytes accessed | tf_op | source)
XLA Modules:
  0.0 25.1 jit_solution(6696339592655019641)
XLA Ops:
  0.0 24.3 %predict.1 = f32[2,128,512]{2,1,0:T(8,128)S(1)} custom-call(s32[16]{0:T(128)} %plan_hbm.1, f32[2]{0:T(128)} %scale_hbm.1, s32[8,512]{1,0:T(8,128)} %constant.6.clone.where_hbm, s32[1,128]{1,0:T(1,128)} %bitcast.3, f32[2,128,512]{2,1,0:T(8,128)} %data_hbm.1, bf16[512,256]{1,0:T(8,128)(2,1)} %bitcast.2, bf16[512,768]{1,0:T(8,128)(2,1)} %constant.7.clone.forward_hbm, ...), custom_call_target="tpu_custom_call" | custom-call | tf_op jit(solution)/shard_map/predict/pallas_call | solution.py:412
  24.3 0.8 %copy.10 = f32[2,128,512]{2,1,0:T(8,128)} copy(f32[2,128,512]{2,1,0:T(8,128)S(1)} %predict.1) | data formatting | bytes 1048576

commit v3 on v2

--- a/solution.py
+++ b/solution.py
@@ -13,7 +13,6 @@
 MESH = pl.DeviceIdType.MESH
 F32 = jnp.float32
 BF16 = jnp.bfloat16
-UNROLL = 16
 BLOCK = 16
 
 
@@ -53,13 +52,15 @@
     side = shot // 2 % 2
     height = shot // 4
     mate = (height * 2 + side) * 2 + 1 - core
-    across = (height * 2 + 1 - side) * 2 + core
+
+    def across(n):
+        return (height * 2 + 1 - side) * 2 + (core + n) % 2
 
     def line(z):
         return (z * 2 + side) * 2 + core
 
     barrier = pltpu.get_barrier_semaphore()
-    for to in (across, mate):
+    for to in (across(0), across(1), mate):
         pl.semaphore_signal(barrier, inc=1, device_id=(to, surf), device_id_type=MESH)
     for z in range(heights):
         for h in range(surfs):
@@ -95,17 +96,17 @@
     def y_copy(n):
         return pltpu.make_async_remote_copy(
             src_ref=primaries_hbm.at[rows_of(n)],
-            dst_ref=panels.at[2, rows_of(n)],
+            dst_ref=panels.at[2 + n % 2, rows_of(n)],
             send_sem=y_send.at[n],
             recv_sem=y_recv.at[n],
-            device_id=(across, surf),
+            device_id=(across(n), surf),
             device_id_type=MESH,
         )
 
     def relay_copy(n):
         return pltpu.make_async_remote_copy(
-            src_ref=panels.at[2, rows_of(n)],
-            dst_ref=panels.at[3, rows_of(n)],
+            src_ref=panels.at[2 + n % 2, rows_of(n)],
+            dst_ref=panels.at[3 - n % 2, rows_of(n)],
             send_sem=relay_send.at[n],
             recv_sem=relay_recv.at[n],
             device_id=(mate, surf),
@@ -202,62 +203,42 @@
                     ]
 
     def work(e, k, pair):
-        def one_tile(f, inner):
-            lanes = pl.ds(pl.multiple_of(f * 128, 128), 128)
-            tiles = 2 * width // 8
-
-            def positions(n, sums):
-                sums = list(sums)
-                for j in range(UNROLL):
-                    x = n * UNROLL + j
-                    rows = [
-                        [
-                            jnp.broadcast_to(
-                                factors.at[k, f, s * 3 + m, pl.ds(pl.multiple_of(n * UNROLL, UNROLL), UNROLL)][j:j + 1],
-                                (8, 128),
-                            )
-                            for m in range(3)
-                        ]
-                        for s in range(shots)
-                    ]
-                    for t in range(tiles):
-                        b, q = t * 8 // width, t * 8 % width
-                        for m, ref in enumerate((e1, e2, e3)):
-                            factor = ref[pair, f, x, b, q:q + 8]
-                            for s in range(shots):
-                                at = (s * 3 + m) * tiles + t
-                                sums[at] = sums[at] + factor * rows[s][m]
-                return tuple(sums)
-
-            zero = jnp.zeros((8, 128), F32)
-            sums = lax.fori_loop(
-                0, depth // UNROLL, positions, (zero,) * (3 * shots * tiles)
-            )
-            k1, k2, k3 = [
-                [
+        tiles = 2 * width // 8
+        first = lax.broadcasted_iota(jnp.int32, (2 * width, 128), 1) == 0
+        back = None
+        for f in range(tiles_f):
+            sums = [None] * (3 * shots * tiles)
+            for x in range(depth):
+                rows = [
+                    jnp.broadcast_to(factors[k, f, n, x:x + 1], (8, 128)) for n in range(3 * shots)
+                ]
+                for t in range(tiles):
+                    b, q = t * 8 // width, t * 8 % width
+                    for m, ref in enumerate((e1, e2, e3)):
+                        factor = ref[pair, f, x, b, q:q + 8]
+                        for s in range(shots):
+                            at = (s * 3 + m) * tiles + t
+                            term = factor * rows[s * 3 + m]
+                            sums[at] = term if sums[at] is None else sums[at] + term
+            for s in range(shots):
+                k1, k2, k3 = [
                     jnp.concatenate(sums[(s * 3 + m) * tiles:(s * 3 + m + 1) * tiles], axis=0)
-                    for s in range(shots)
+                    for m in range(3)
                 ]
-                for m in range(3)
-            ]
-            first = lax.broadcasted_iota(jnp.int32, (2 * width, 128), 1) + f * 128 == 0
-            imag_lanes = pl.ds(pl.multiple_of(half + f * 128, 128), 128)
-            for s in range(shots):
-                re = jnp.where(first, k2[s], k1[s] - k3[s])
-                im = jnp.where(first, k3[s], k1[s] + k2[s])
+                re, im = k1 - k3, k1 + k2
+                if f == 0:
+                    re, im = jnp.where(first, k2, re), jnp.where(first, k3, im)
                 for h in range(surfs):
                     for b in range(2):
                         low = ((h * shots + s) * 2 + b) * per_surf
                         src = b * width + h * per_surf
-                        spectrum[low:low + per_surf, lanes] = re[src:src + per_surf]
-                        spectrum[low:low + per_surf, imag_lanes] = im[src:src + per_surf]
-            return inner
-
-        lax.fori_loop(0, tiles_f, one_tile, 0)
-        back = jnp.dot(spectrum[...].astype(BF16), inverse_ref[...], preferred_element_type=F32)
-        rows = shots * 2 * per_surf
+                        spectrum[low:low + per_surf, f * 256:f * 256 + 128] = re[src:src + per_surf]
+                        spectrum[low:low + per_surf, f * 256 + 128:f * 256 + 256] = im[src:src + per_surf]
+            lanes = slice(f * 256, f * 256 + 256)
+            part = jnp.dot(spectrum[:, lanes].astype(BF16), inverse_ref[lanes, :], preferred_element_type=F32)
+            back = part if back is None else back + part
         for h in range(surfs):
-            leaving[e, h] = back[h * rows:(h + 1) * rows].astype(BF16)
+            leaving[e, h] = back[h * rows_item:(h + 1) * rows_item].astype(BF16)
         for h in range(surfs):
 
             @pl.when((k != 0) | (h != surf))
@@ -268,7 +249,7 @@
         def _():
             own_copy(pair).start()
 
-    pl.semaphore_wait(barrier, heights * surfs + 1)
+    pl.semaphore_wait(barrier, heights * surfs + 2)
     mate_copy.start()
     for k in range(1, heights):
         g_copy(order(k)).start()
@@ -294,9 +275,10 @@
     panel_spectra(1, 0, 1, 0, depth)
 
     def take_piece(n):
-        pltpu.make_async_copy(panels.at[2, rows_of(n)], panels.at[2, rows_of(n)], y_recv.at[n]).wait()
+        piece = panels.at[2 + n % 2, rows_of(n)]
+        pltpu.make_async_copy(piece, piece, y_recv.at[n]).wait()
         relay_copy(n).start()
-        panel_spectra(2, 1, 0, n, BLOCK)
+        panel_spectra(2 + n % 2, 1, n % 2, n, BLOCK)
 
     work(0, 0, 0)
 
@@ -317,8 +299,9 @@
     lax.fori_loop(1, pieces, y_piece, 0)
 
     def relayed_piece(n, carry):
-        pltpu.make_async_copy(panels.at[3, rows_of(n)], panels.at[3, rows_of(n)], relay_recv.at[n]).wait()
-        panel_spectra(3, 1, 1, n, BLOCK)
+        piece = panels.at[3 - n % 2, rows_of(n)]
+        pltpu.make_async_copy(piece, piece, relay_recv.at[n]).wait()
+        panel_spectra(3 - n % 2, 1, 1 - n % 2, n, BLOCK)
         return carry
 
     lax.fori_loop(0, pieces, relayed_piece, 0)
@@ -390,6 +373,7 @@
     per_surf = width // surfs
     half = -(-(samples + taps - 1) // 256) * 128
     forward, inverse = fourier_matrices(samples, 2 * half)
+    inverse = inverse.reshape(2, half // 128, 128, samples).transpose(1, 0, 2, 3).reshape(inverse.shape)
     rows = shots * 2 * per_surf
     items = 2 * heights
     pieces = depth // BLOCK

time: 25.2 us -> 25.3 us (level)
  no operation moved by 1% of the time
where the time goes in v3:
time: 25.3 us; the launch traced here: 25 us
  Pallas kernels  24.2 us (96%)
  local copies, waits for them, and re-layouts  0.8 us (3%)
    pallas_call x1, Pallas kernels, on_device(): pl.pallas_call(functools.partial(predict_kernel, sizes), out_shape=pltpu....  24.2 us
    unnamed x1, local copies, waits for them, and re-layouts  0.8 us

profile of v3, /device:TPU:0, one launch (start us, length us, event | category | flops | bytes accessed | tf_op | source)
XLA Modules:
  0.0 25.0 jit_solution(7770081752871773652)
XLA Ops:
  0.0 24.2 %predict.1 = f32[2,128,512]{2,1,0:T(8,128)S(1)} custom-call(s32[16]{0:T(128)} %plan_hbm.1, f32[2]{0:T(128)} %scale_hbm.1, s32[8,512]{1,0:T(8,128)} %constant.6.clone.where_hbm, s32[1,128]{1,0:T(1,128)} %bitcast.3, f32[2,128,512]{2,1,0:T(8,128)} %data_hbm.1, bf16[512,256]{1,0:T(8,128)(2,1)} %bitcast.2, bf16[512,768]{1,0:T(8,128)(2,1)} %constant.7.clone.forward_hbm, ...), custom_call_target="tpu_custom_call" | custom-call | tf_op jit(solution)/shard_map/predict/pallas_call | solution.py:396
  24.2 0.8 %copy.10 = f32[2,128,512]{2,1,0:T(8,128)} copy(f32[2,128,512]{2,1,0:T(8,128)S(1)} %predict.1) | data formatting | bytes 1048576

commit v4 on v2

--- a/solution.py
+++ b/solution.py
@@ -13,7 +13,7 @@
 MESH = pl.DeviceIdType.MESH
 F32 = jnp.float32
 BF16 = jnp.bfloat16
-UNROLL = 16
+UNROLL = 32
 BLOCK = 16
 
 

time: 25.2 us -> 26.1 us (1.036)
  Pallas kernels: 24.3 us -> 25.2 us
    pallas_call x1, Pallas kernels: 24.3 us -> 25.2 us  [on_device(): pl.pallas_call(functools.partial(predict_kernel, sizes), out_shape=pltpu....]
where the time goes in v4:
time: 26.1 us; the launch traced here: 26 us
  Pallas kernels  25.2 us (97%)
  local copies, waits for them, and re-layouts  0.8 us (3%)
    pallas_call x1, Pallas kernels, on_device(): pl.pallas_call(functools.partial(predict_kernel, sizes), out_shape=pltpu....  25.2 us
    unnamed x1, local copies, waits for them, and re-layouts  0.8 us

profile of v4, /device:TPU:0, one launch (start us, length us, event | category | flops | bytes accessed | tf_op | source)
XLA Modules:
  0.0 26.0 jit_solution(6595028525498801139)
XLA Ops:
  0.0 25.2 %predict.1 = f32[2,128,512]{2,1,0:T(8,128)S(1)} custom-call(s32[16]{0:T(128)} %plan_hbm.1, f32[2]{0:T(128)} %scale_hbm.1, s32[8,512]{1,0:T(8,128)} %constant.6.clone.where_hbm, s32[1,128]{1,0:T(1,128)} %bitcast.3, f32[2,128,512]{2,1,0:T(8,128)} %data_hbm.1, bf16[512,256]{1,0:T(8,128)(2,1)} %bitcast.2, bf16[512,768]{1,0:T(8,128)(2,1)} %constant.7.clone.forward_hbm, ...), custom_call_target="tpu_custom_call" | custom-call | tf_op jit(solution)/shard_map/predict/pallas_call | solution.py:412
  25.2 0.8 %copy.10 = f32[2,128,512]{2,1,0:T(8,128)} copy(f32[2,128,512]{2,1,0:T(8,128)S(1)} %predict.1) | data formatting | bytes 1048576
